TPU v7x, 256 devices: a whole 4x4x8 slice. The times are simulated.
256 devices in a mesh: strip: 64 (over z, x, core), frame: 4 (over y).
Axes of the slice: x: 4, y: 4, z: 8, core: 2. Of those that a mesh axis runs over, the one named last changes fastest.
Arguments:
- frames_in: bfloat16 [4, 256, 240, 768], P('frame', 'strip'), may hold values from -6 to 6
- dw_weight: float32 [7, 7, 768], replicated, may hold values from -0.875 to 0.875
- dw_bias: float32 [768], replicated, may hold values from -4 to 4
- ln_gain: float32 [768], replicated, may hold values from 0.5 to 2
- ln_bias: float32 [768], replicated, may hold values from -3 to 3
- w_in: bfloat16 [768, 3072], replicated, may hold values from -0.21875 to 0.21875
- b_in: float32 [3072], replicated, may hold values from -3 to 3
- w_out: bfloat16 [3072, 768], replicated, may hold values from -0.109375 to 0.109375
- b_out: float32 [768], replicated, may hold values from -3 to 3
- layer_scale: float32 [768], replicated, may hold values from 0.3 to 1.5
- depth_bins: int32 [4, 256, 240], P('frame', 'strip'), may hold values from -1 to 111, as said below
- return_counts: int32 [4, 256, 240], P('frame', 'strip'), may hold values from 1 to 4
Outputs:
- features: bfloat16 [4, 256, 240, 768], P('frame', 'strip')
- probe_stat: float32 [768, 112], replicated
Inputs may be any that keep to these rules, and one draw needn't show every extreme that they name: `depth_bins`: every row of every frame has at least one pixel with a return.
All inputs are finite; a program needn't handle non-finite values.
Results may differ from a plain program's by a relative error of at most 0.0056.
Values may be sent and summed in bfloat16 or wider, within the bound.
No kernel may reach another device: no remote copies, remote signals or barrier semaphores. Data moves between devices by JAX's collectives and lax.ppermute only.
A program may use at most 128 MiB of HBM per device.

v0:
```python
import functools
import jax
import jax.numpy as jnp
from jax import lax
from jax.experimental import pallas as pl
from jax.experimental.pallas import tpu as pltpu
from jax.sharding import PartitionSpec as P

BINS = 112
C = 768
NB = C // 128
TRI = [(i, j) for i in range(NB) for j in range(i, NB)]
XY0 = len(TRI) * 128
ROWS = XY0 + C
PACK = 3584
ridge = 0.05

VMEM = pl.BlockSpec(memory_space=pltpu.VMEM)

F32 = jnp.float32
BF = jnp.bfloat16


def strip_id(z, x, c):
    return ((z % 8) * 4 + (x % 4)) * 2 + c


ALL = [(z, x, c) for z in range(8) for x in range(4) for c in range(2)]
CORE = [(strip_id(z, x, c), strip_id(z, x, 1 - c)) for z, x, c in ALL]


def x_shift(k):
    return [(strip_id(z, x, c), strip_id(z, x + k, c)) for z, x, c in ALL]


def z_flip(m):
    return [(strip_id(z, x, c), strip_id(z ^ m, x, c)) for z, x, c in ALL]


def y_shift(k):
    return [(i, (i + k) % 4) for i in range(4)]


def chunk(arr, at, size):
    return lax.dynamic_slice_in_dim(arr, at * size, size, axis=0)


def scatter4(arr, axis, pairs, me):
    size = arr.shape[0] // 4
    out = chunk(arr, me, size)
    for k in (2, 1, 3):
        out = out + lax.ppermute(chunk(arr, (me + k) % 4, size), axis, pairs(k))
    return out


def gather4(arr, axis, pairs, me):
    size = arr.shape[0]
    out = jnp.zeros((4 * size, arr.shape[1]), arr.dtype)
    got = [(k, lax.ppermute(arr, axis, pairs(k))) for k in (2, 1, 3)]
    out = lax.dynamic_update_slice_in_dim(out, arr, me * size, axis=0)
    for k, piece in got:
        out = lax.dynamic_update_slice_in_dim(out, piece, ((me + 4 - k) % 4) * size, axis=0)
    return out


def sum_devices(arr):
    strip = lax.axis_index("strip")
    y = lax.axis_index("frame")
    c = strip % 2
    x = (strip // 2) % 4
    half = arr.shape[0] // 2
    arr = chunk(arr, c, half) + lax.ppermute(chunk(arr, 1 - c, half), "strip", CORE)
    arr = scatter4(arr, "frame", y_shift, y)
    arr = scatter4(arr, "strip", x_shift, x)
    near = {m: lax.ppermute(arr, "strip", z_flip(m)) for m in (3, 2, 1)}
    arr = (arr + near[1]) + (near[2] + near[3])
    arr = arr + lax.ppermute(arr, "strip", z_flip(7))
    arr = gather4(arr, "strip", x_shift, x)
    arr = gather4(arr, "frame", y_shift, y)
    other = lax.ppermute(arr, "strip", CORE)
    return jnp.where(c == 0, jnp.concatenate([arr, other]), jnp.concatenate([other, arr]))


def split(v):
    hi = v.astype(BF)
    return hi, (v - hi.astype(F32)).astype(BF)


def split3(v):
    hi = v.astype(BF)
    rest = v - hi.astype(F32)
    lo = rest.astype(BF)
    return hi, lo, (rest - lo.astype(F32)).astype(BF)


def col_sum(v):
    return jnp.sum(v, axis=0, keepdims=True)


def solve_kernel(g_ref, out_ref, lo2_ref, hi_ref, lo_ref, b_ref, x_ref, r_ref, d_ref, p_ref, q_ref, cat_ref):
    lane = lax.broadcasted_iota(jnp.int32, (1, 128), 1)
    total = jnp.max(g_ref[XY0 + BINS : XY0 + BINS + 1, :])
    eye = jnp.where(
        lax.broadcasted_iota(jnp.int32, (128, 128), 0) == lax.broadcasted_iota(jnp.int32, (128, 128), 1), ridge, 0.0
    ).astype(F32)
    for t, (i, j) in enumerate(TRI):
        blk = g_ref[t * 128 : (t + 1) * 128, :] / total
        if i == j:
            blk = blk + eye
        ri, rj = slice(i * 128, (i + 1) * 128), slice(j * 128, (j + 1) * 128)
        hi_ref[ri, rj], lo_ref[ri, rj], lo2_ref[ri, rj] = split3(blk)
        if i != j:
            hi_ref[rj, ri], lo_ref[rj, ri], lo2_ref[rj, ri] = split3(blk.T)
    for i in range(NB):
        blk = g_ref[XY0 + i * 128 : XY0 + (i + 1) * 128, :].T / total
        b_ref[i * 128 : (i + 1) * 128, :] = jnp.where(lane < BINS, blk, 0.0)
    b = b_ref[...]
    r_ref[...] = b
    x_ref[...] = jnp.zeros((C, 128), F32)
    bb = col_sum(b * b)
    safe_bb = jnp.where(bb > 0, bb, 1.0)

    def inner_cond(s):
        return (s[1] > 1.0) & (s[0] < 2000)

    def rounds_cond(s):
        return (s[1] > 1.0) & (s[0] < 40)

    def rounds(s):
        n, worst = s
        r = r_ref[...]
        rr0 = col_sum(r * r)
        goal = jnp.maximum(rr0 * INNER2, bb * FINAL2 * 0.25)
        goal = jnp.where(goal > 0, goal, 1.0)
        d_ref[...] = jnp.zeros((C, 128), F32)
        p_ref[...] = r

        def inner(t):
            it, _, rr = t
            p = p_ref[...]
            hi, lo = split(p)
            cat_ref[:, :128] = hi
            cat_ref[:, 128:] = lo
            cat = cat_ref[...]
            pap = jnp.zeros((1, 128), F32)
            for m in range(2):
                rows = slice(m * 384, (m + 1) * 384)
                q = jnp.dot(hi_ref[rows, :], cat, preferred_element_type=F32) + jnp.dot(
                    lo_ref[rows, :], cat, preferred_element_type=F32
                )
                q = q[:, :128] + q[:, 128:]
                q_ref[rows, :] = q
                pap = pap + col_sum(q * p_ref[rows, :])
            alpha = jnp.where(pap > 0, rr / jnp.where(pap > 0, pap, 1.0), 0.0)
            r = r_ref[...] - alpha * q_ref[...]
            r_ref[...] = r
            d_ref[...] = d_ref[...] + alpha * p
            new = col_sum(r * r)
            beta = jnp.where(rr > 0, new / jnp.where(rr > 0, rr, 1.0), 0.0)
            p_ref[...] = r + beta * p
            return it + 1, jnp.max(new / goal), new

        lax.while_loop(inner_cond, inner, (jnp.int32(0), jnp.float32(2.0), rr0))
        x = x_ref[...] + d_ref[...]
        x_ref[...] = x
        hi, lo, lo2 = split3(x)
        cat_ref[:, :128] = hi
        cat_ref[:, 128:] = lo
        cat = cat_ref[...]
        for m in range(3):
            rows = slice(m * 256, (m + 1) * 256)
            q = jnp.dot(lo2_ref[rows, :], cat, preferred_element_type=F32)
            q = q + jnp.dot(lo_ref[rows, :], cat, preferred_element_type=F32)
            q = q + jnp.dot(hi_ref[rows, :], cat, preferred_element_type=F32)
            q_ref[rows, :] = q[:, :128] + (
                q[:, 128:] + jnp.dot(hi_ref[rows, :], lo2, preferred_element_type=F32)
            )
        r = b_ref[...] - q_ref[...]
        r_ref[...] = r
        now = jnp.max(col_sum(r * r) / (safe_bb * FINAL2))
        go = (now > 1.0) & (now < 0.25 * worst)
        return n + 1, jnp.where(go, now, 0.0)

    lax.while_loop(rounds_cond, rounds, (jnp.int32(0), jnp.float32(3.0e38)))
    scale = jnp.sqrt(jnp.full((1, 128), total * BINS, F32))
    out_ref[...] = (x_ref[...] * scale)[:, :BINS]


INNER2 = 1e-8
FINAL2 = 1e-12


def solve(packed):
    mat = pltpu.VMEM((C, 128), F32)
    return pl.pallas_call(
        solve_kernel,
        out_shape=jax.ShapeDtypeStruct((C, BINS), F32),
        in_specs=[VMEM],
        out_specs=VMEM,
        scratch_shapes=[
            pltpu.VMEM((C, C), BF),
            pltpu.VMEM((C, C), BF),
            pltpu.VMEM((C, C), BF),
            mat, mat, mat, mat, mat, mat,
            pltpu.VMEM((C, 256), BF),
        ],
        compiler_params=pltpu.CompilerParams(vmem_limit_bytes=48 * 1024 * 1024),
        name="ridge_solve",
    )(packed)


W = 240
HID = 3072
NJ = W // 8
PJ = NJ + 6
PIX = 1024


def orders():
    p = lax.broadcasted_iota(jnp.int32, (PJ * 8, W), 0)
    w = lax.broadcasted_iota(jnp.int32, (PJ * 8, W), 1)
    spread = (w == (p % 8) * NJ + p // 8 - 3).astype(BF)
    w = lax.broadcasted_iota(jnp.int32, (W, W), 0)
    p = lax.broadcasted_iota(jnp.int32, (W, W), 1)
    back = (w == (p % 8) * NJ + p // 8).astype(BF)
    return spread, back


ATANH_ERF = [0.7978842690838895, 0.03633414661429164, -3.302471253972585e-05, -5.527399961498717e-05, 3.974156182767768e-06, -1.3378855696121708e-07, 1.814048873178476e-09]


def gelu_half(half):
    sq = half * half
    poly = ATANH_ERF[-1] * 2.0 * 4.0 ** (len(ATANH_ERF) - 1)
    for k in range(len(ATANH_ERF) - 2, -1, -1):
        poly = poly * sq + ATANH_ERF[k] * 2.0 * 4.0**k
    return half + half * jnp.tanh(half * poly)


def spread_weights(dw, dwb):
    for k in range(49):
        dwb[k] = jnp.broadcast_to(dw[k : k + 1, :], (8, C))


def add_rows(xs, dwb, sums, at, lanes, rows):
    for slot, r in rows:
        x = xs[slot, pl.ds(at, 12), :, lanes]
        for b in range(7):
            xb = x[b : b + 6]
            for h in range(4):
                if 0 <= r - h < 7:
                    sums[h] = sums[h] + xb * dwb[(r - h) * 7 + b, :, lanes][None]
    return sums


OWN_ROWS = [(k, 3 + k) for k in range(4)]
HALO_ROWS = [(k, k if k < 3 else 4 + k) for k in range(6)]


def bring_row(r, xin, xs, spread):
    xs[r] = jnp.dot(spread[...], xin[r], preferred_element_type=F32).reshape(PJ, 8, C)


def own_kernel(own, dw, vec, spread, acc, was, xin, xs, dwb, sems):
    copy = pltpu.make_async_copy(own, xin, sems.at[0])
    copy.start()
    spread_weights(dw, dwb)
    copy.wait()

    def bring(r, _):
        bring_row(r, xin, xs, spread)
        was[pl.ds(pl.multiple_of(r * W, W), W), :] = xs[r, 3 : 3 + NJ].reshape(W, C).astype(BF)
        return 0

    lax.fori_loop(0, 4, bring, 0)

    def conv(t, _):
        lanes = pl.ds(pl.multiple_of((t // 5) * 128, 128), 128)
        at = (t % 5) * 6
        bias = jnp.broadcast_to(vec[0:1, lanes], (6, 8, 128))
        sums = add_rows(xs, dwb, [bias, bias, bias, bias], at, lanes, OWN_ROWS)
        for h in range(4):
            acc[h, pl.ds(at, 6), :, lanes] = sums[h]
        return 0

    lax.fori_loop(0, 30, conv, 0)


def block_kernel(
    part, was_in, top, bot, dw, vec, b_in, spread, back, bins, counts, w_in, w_out,
    feat, packed,
    xin, xs, dwb, acc, was, normed, hid, f_ref, odd, even, win, wout, sems,
):
    copies = [
        pltpu.make_async_copy(top, xin.at[pl.ds(0, 3)], sems.at[0]),
        pltpu.make_async_copy(bot, xin.at[pl.ds(3, 3)], sems.at[1]),
        pltpu.make_async_copy(part, acc, sems.at[2]),
        pltpu.make_async_copy(w_in, win, sems.at[3]),
        pltpu.make_async_copy(w_out, wout, sems.at[4]),
        pltpu.make_async_copy(was_in, was, sems.at[5]),
    ]
    for copy in copies:
        copy.start()
    spread_weights(dw, dwb)
    for copy in copies[:2]:
        copy.wait()

    def bring(r, _):
        bring_row(r, xin, xs, spread)
        return 0

    lax.fori_loop(0, 6, bring, 0)
    copies[2].wait()

    def conv(t, _):
        lanes = pl.ds(pl.multiple_of((t // 5) * 128, 128), 128)
        at = (t % 5) * 6
        sums = [acc[h, pl.ds(at, 6), :, lanes] for h in range(4)]
        sums = add_rows(xs, dwb, sums, at, lanes, HALO_ROWS)
        for h in range(4):
            acc[h, pl.ds(at, 6), :, lanes] = sums[h]
        return 0

    lax.fori_loop(0, 30, conv, 0)

    def norm(h, _):
        v = acc[h].reshape(W, C)
        mean = jnp.mean(v, axis=1, keepdims=True)
        v = v - mean
        var = jnp.mean(v * v, axis=1, keepdims=True)
        v = v * lax.rsqrt(var + 1e-06) * vec[1:2, :] + vec[2:3, :]
        normed[pl.ds(pl.multiple_of(h * W, W), W), :] = v.astype(BF)
        return 0

    lax.fori_loop(0, 4, norm, 0)
    copies[3].wait()

    def up(n, _):
        cols = pl.ds(pl.multiple_of(n * 256, 256), 256)
        h = jnp.dot(normed[...], win[:, cols], preferred_element_type=F32) + b_in[:, cols]
        hid[:, cols] = gelu_half(h).astype(BF)
        return 0

    lax.fori_loop(0, HID // 256, up, 0)
    copies[4].wait()
    copies[5].wait()
    f_ref[4 * W :, :] = jnp.zeros((PIX - 4 * W, C), BF)

    def down(n, _):
        cols = pl.ds(pl.multiple_of(n * 256, 256), 256)
        branch = jnp.dot(hid[...], wout[:, cols], preferred_element_type=F32) + vec[3:4, cols]
        f_ref[: 4 * W, cols] = (was[:, cols].astype(F32) + vec[4:5, cols] * branch).astype(BF)
        return 0

    lax.fori_loop(0, C // 256, down, 0)

    def order(m, _):
        rows = pl.ds(pl.multiple_of(m * W, W), W)
        feat[m] = jnp.dot(back[...], f_ref[rows, :], preferred_element_type=F32).astype(BF)
        return 0

    lax.fori_loop(0, 4, order, 0)

    weight = jnp.where(bins[...] >= 0, counts[...], 0)
    odd_w = weight % 2
    even_w = (weight - odd_w).astype(F32)
    odd_w = odd_w.astype(F32)
    for i in range(NB):
        flip = f_ref[:, i * 128 : (i + 1) * 128].astype(F32).T
        odd[...] = (flip * odd_w).astype(BF)
        even[...] = (flip * even_w).astype(BF)
        side = f_ref[:, i * 128 :]
        gram = jnp.dot(odd[...], side, preferred_element_type=F32) + jnp.dot(
            even[...], side, preferred_element_type=F32
        )
        for j in range(i, NB):
            t = TRI.index((i, j))
            packed[t * 128 : (t + 1) * 128, :] = gram[:, (j - i) * 128 : (j - i + 1) * 128]
    hot = lax.broadcasted_iota(jnp.int32, (128, PIX), 0) == bins[...]
    hot = jnp.where(hot, weight, 0).astype(F32).astype(BF)
    xy = jnp.dot(hot, f_ref[...], preferred_element_type=F32)
    total = jnp.sum(weight.astype(F32), axis=1, keepdims=True)
    xy = jnp.where(lax.broadcasted_iota(jnp.int32, (128, C), 0) == BINS, total, xy)
    for i in range(NB):
        packed[XY0 + i * 128 : XY0 + (i + 1) * 128, :] = xy[:, i * 128 : (i + 1) * 128]
    packed[ROWS:, :] = jnp.zeros((PACK - ROWS, 128), F32)


def run_own(own, dw, vec, spread):
    part = jax.ShapeDtypeStruct((4, NJ, 8, C), F32)
    was = jax.ShapeDtypeStruct((4 * W, C), BF)
    return pl.pallas_call(
        own_kernel,
        out_shape=(part, was),
        in_specs=[pl.BlockSpec(memory_space=pl.ANY)] + [VMEM] * 3,
        out_specs=(VMEM, VMEM),
        scratch_shapes=[
            pltpu.VMEM((4, W, C), BF),
            pltpu.VMEM((4, PJ, 8, C), F32),
            pltpu.VMEM((49, 8, C), F32),
            pltpu.SemaphoreType.DMA((1,)),
        ],
        compiler_params=pltpu.CompilerParams(vmem_limit_bytes=24 * 1024 * 1024),
        cost_estimate=pl.CostEstimate(flops=6_000_000_000, bytes_accessed=12_000_000, transcendentals=0),
        name="own_rows",
    )(own, dw, vec, spread)


def run_block(own, top, bot, dw, vec, b_in, bins, counts, w_in, w_out):
    spread, back = orders()
    part, was = run_own(own, dw, vec, spread)
    anyspec = pl.BlockSpec(memory_space=pl.ANY)
    return pl.pallas_call(
        block_kernel,
        out_shape=(jax.ShapeDtypeStruct(own.shape, BF), jax.ShapeDtypeStruct((PACK, 128), F32)),
        in_specs=[anyspec] * 4 + [VMEM] * 7 + [anyspec] * 2,
        out_specs=(VMEM, VMEM),
        scratch_shapes=[
            pltpu.VMEM((6, W, C), BF),
            pltpu.VMEM((6, PJ, 8, C), F32),
            pltpu.VMEM((49, 8, C), F32),
            pltpu.VMEM((4, NJ, 8, C), F32),
            pltpu.VMEM((4 * W, C), BF),
            pltpu.VMEM((4 * W, C), BF),
            pltpu.VMEM((4 * W, HID), BF),
            pltpu.VMEM((PIX, C), BF),
            pltpu.VMEM((128, PIX), BF),
            pltpu.VMEM((128, PIX), BF),
            pltpu.VMEM((C, HID), BF),
            pltpu.VMEM((HID, C), BF),
            pltpu.SemaphoreType.DMA((6,)),
        ],
        compiler_params=pltpu.CompilerParams(vmem_limit_bytes=48 * 1024 * 1024),
        name="block",
    )(part, was, top, bot, dw, vec, b_in, spread, back, bins, counts, w_in, w_out)


def pixel_row(arr, fill):
    arr = arr.reshape(4, 8, NJ).transpose(0, 2, 1).reshape(1, 4 * W)
    return jnp.pad(arr, ((0, 0), (0, PIX - 4 * W)), constant_values=fill)


def per_device(
    frames_in, dw_weight, dw_bias, ln_gain, ln_bias, w_in, b_in, w_out, b_out, layer_scale, depth_bins, return_counts
):
    own = frames_in[0]
    ends = lax.axis_size("strip") - 1
    bot = lax.ppermute(own[:3], "strip", [(i + 1, i) for i in range(ends)])
    top = lax.ppermute(own[1:], "strip", [(i, i + 1) for i in range(ends)])
    vec = jnp.stack([dw_bias, 0.5 * ln_gain, 0.5 * ln_bias, b_out, layer_scale, b_out, b_out, b_out])
    features, packed = run_block(
        own, top, bot, dw_weight.reshape(49, C), vec, 0.5 * b_in.reshape(1, HID),
        pixel_row(depth_bins[0], -1), pixel_row(return_counts[0], 0), w_in, w_out,
    )
    return (features[None], solve(sum_devices(packed)))


def solution(mesh):
    placed = (
        P("frame", "strip", None, None),
        P(),
        P(),
        P(),
        P(),
        P(),
        P(),
        P(),
        P(),
        P(),
        P("frame", "strip", None),
        P("frame", "strip", None),
    )
    return jax.shard_map(
        per_device,
        mesh=mesh,
        in_specs=placed,
        out_specs=(P("frame", "strip", None, None), P()),
        check_vma=False,
    )
```

profile of v0, /device:TPU:1, one launch (start us, length us, event | category | flops | bytes accessed | tf_op | source)
XLA Modules:
  0.0 164.6 jit_solution(11077123192134892901)
XLA Ops:
  0.7 3.2 %slice_bitcast_fusion = (bf16[3,240,768]{2,1,0:T(8,128)(2,1)}, bf16[3,240,768]{2,1,0:T(8,128)(2,1)}) fusion(bf16[1,4,240,768]{3,2,1,0:T(8,128)(2,1)} %param.12), kind=kLoop, calls=%fused_computation.1 | loop fusion | bytes 4423680 | tf_op jit(solution)/shard_map/slice | solution.py:448
  3.9 4.5 %collective-permute-start = (bf16[3,240,768]{2,1,0:T(8,128)(2,1)}, bf16[3,240,768]{2,1,0:T(8,128)(2,1)S(1)}, u32[]{:S(2)}, u32[]{:S(2)}) collective-permute-start(bf16[3,240,768]{2,1,0:T(8,128)(2,1)} %get-tuple-element.17), channel_id=1, source_target_pairs={{0,4},{4,8},{8,12},{12,16},{16,20},{20,24},{24,28},{28,32},{32,36}... | collective-permute-start | bytes 3317768 | tf_op jit(solution)/shard_map/ppermute | solution.py:449
  8.4 2.0 %collective-permute-start.1 = (bf16[3,240,768]{2,1,0:T(8,128)(2,1)}, bf16[3,240,768]{2,1,0:T(8,128)(2,1)}, u32[]{:S(2)}, u32[]{:S(2)}) collective-permute-start(bf16[3,240,768]{2,1,0:T(8,128)(2,1)} %get-tuple-element.16), channel_id=1, source_target_pairs={{4,0},{8,4},{12,8},{16,12},{20,16},{24,20},{28,24},{32,28},{36,32}... | collective-permute-start | bytes 3317768 | tf_op jit(solution)/shard_map/ppermute | solution.py:448
  11.7 7.9 %own_rows.1 = (f32[4,30,8,768]{3,2,1,0:T(8,128)S(1)}, bf16[960,768]{1,0:T(8,128)(2,1)S(1)}) custom-call(bf16[4,240,768]{2,1,0:T(8,128)(2,1)S(1)} %bitcast.9, f32[49,768]{1,0:T(8,128)S(1)} %reshape.17.dw, f32[8,768]{1,0:T(8,128)S(1)} %stack.26.vec, bf16[288,240]{1,0:T(8,128)(2,1)S(1)} %fusion.spread), custom_call_target="tpu_custom_call" | custom-call | flops 6000000000 | bytes 12000000 | tf_op jit(solution)/shard_map/own_rows/pallas_call | solution.py:392
  21.2 4.3 %collective-permute-done.1.bot = bf16[3,240,768]{2,1,0:T(8,128)(2,1)} collective-permute-done((bf16[3,240,768]{2,1,0:T(8,128)(2,1)}, bf16[3,240,768]{2,1,0:T(8,128)(2,1)}, u32[]{:S(2)}, u32[]{:S(2)}) %collective-permute-start.1) | collective-permute-done | bytes 1105952 | tf_op jit(solution)/shard_map/ppermute | solution.py:448
  25.4 28.5 %block.1 = (bf16[4,240,768]{2,1,0:T(8,128)(2,1)}, f32[3584,128]{1,0:T(8,128)S(1)}) custom-call(f32[4,30,8,768]{3,2,1,0:T(8,128)} %copy-done.1, bf16[960,768]{1,0:T(8,128)(2,1)S(1)} %get-tuple-element.7.was_in, bf16[3,240,768]{2,1,0:T(8,128)(2,1)S(1)} %collective-permute-done.top, bf16[3,240,768]{2,1,0:T(8,128)(2,1)} %collective-permute-done.1.bot, ...), custom_call_target="tpu_custom_call" | custom-call | tf_op jit(solution)/shard_map/block/pallas_call | solution.py:413
  54.2 2.5 %collective-permute-done.2 = f32[1792,128]{1,0:T(8,128)} collective-permute-done((f32[1792,128]{1,0:T(8,128)S(1)}, f32[1792,128]{1,0:T(8,128)}, u32[]{:S(2)}, u32[]{:S(2)}) %collective-permute-start.2) | collective-permute-done | bytes 917536 | tf_op jit(solution)/shard_map/ppermute | solution.py:72
  58.0 2.8 %collective-permute-start.5 = (f32[448,128]{1,0:T(8,128)S(1)}, f32[448,128]{1,0:T(8,128)S(1)}, u32[]{:S(2)}, u32[]{:S(2)}) collective-permute-start(f32[448,128]{1,0:T(8,128)S(1)} %get-tuple-element.19), channel_id=1, source_target_pairs={{0,3},{1,0},{2,1},{3,2},{4,7},{5,4},{6,5},{7,6},{8,11},{9,8},{10,9... | collective-permute-start | bytes 688136 | tf_op jit(solution)/shard_map/ppermute | solution.py:52
  62.5 8.0 %collective-permute-done.5 = f32[448,128]{1,0:T(8,128)S(1)} collective-permute-done((f32[448,128]{1,0:T(8,128)S(1)}, f32[448,128]{1,0:T(8,128)S(1)}, u32[]{:S(2)}, u32[]{:S(2)}) %collective-permute-start.5) | collective-permute-done | bytes 229408 | tf_op jit(solution)/shard_map/ppermute | solution.py:52
  70.5 3.3 %collective-permute-done.4 = f32[448,128]{1,0:T(8,128)S(1)} collective-permute-done((f32[448,128]{1,0:T(8,128)S(1)}, f32[448,128]{1,0:T(8,128)S(1)}, u32[]{:S(2)}, u32[]{:S(2)}) %collective-permute-start.4) | collective-permute-done | bytes 229408 | tf_op jit(solution)/shard_map/ppermute | solution.py:52
  73.8 5.0 %collective-permute-start.8 = (f32[112,128]{1,0:T(8,128)S(1)}, f32[112,128]{1,0:T(8,128)S(1)}, u32[]{:S(2)}, u32[]{:S(2)}) collective-permute-start(f32[112,128]{1,0:T(8,128)S(1)} %get-tuple-element.22), channel_id=1, source_target_pairs={{0,24},{4,28},{8,0},{12,4},{16,8},{20,12},{24,16},{28,20},{32,56},... | collective-permute-start | bytes 172040 | tf_op jit(solution)/shard_map/ppermute | solution.py:52
  80.1 3.3 %collective-permute-done.7 = f32[112,128]{1,0:T(8,128)S(1)} collective-permute-done((f32[112,128]{1,0:T(8,128)S(1)}, f32[112,128]{1,0:T(8,128)S(1)}, u32[]{:S(2)}, u32[]{:S(2)}) %collective-permute-start.7) | collective-permute-done | bytes 57376 | tf_op jit(solution)/shard_map/ppermute | solution.py:52
  84.0 3.3 %collective-permute-start.10 = (f32[112,128]{1,0:T(8,128)S(1)}, f32[112,128]{1,0:T(8,128)S(1)}, u32[]{:S(2)}, u32[]{:S(2)}) collective-permute-start(f32[112,128]{1,0:T(8,128)S(1)} %add_add_fusion.2), channel_id=1, source_target_pairs={{0,64},{4,68},{8,72},{12,76},{16,80},{20,84},{24,88},{28,92},{32,9... | collective-permute-start | bytes 172040 | tf_op jit(solution)/shard_map/ppermute | solution.py:75
  87.2 3.9 %collective-permute-start.11 = (f32[112,128]{1,0:T(8,128)S(1)}, f32[112,128]{1,0:T(8,128)S(1)}, u32[]{:S(2)}, u32[]{:S(2)}) collective-permute-start(f32[112,128]{1,0:T(8,128)S(1)} %add_add_fusion.2), channel_id=1, source_target_pairs={{0,96},{4,100},{8,104},{12,108},{16,112},{20,116},{24,120},{28,124... | collective-permute-start | bytes 172040 | tf_op jit(solution)/shard_map/ppermute | solution.py:75
  91.3 1.9 %collective-permute-done.11 = f32[112,128]{1,0:T(8,128)S(1)} collective-permute-done((f32[112,128]{1,0:T(8,128)S(1)}, f32[112,128]{1,0:T(8,128)S(1)}, u32[]{:S(2)}, u32[]{:S(2)}) %collective-permute-start.11) | collective-permute-done | bytes 57376 | tf_op jit(solution)/shard_map/ppermute | solution.py:75
  94.1 1.7 %collective-permute-start.12 = (f32[112,128]{1,0:T(8,128)S(1)}, f32[112,128]{1,0:T(8,128)S(1)}, u32[]{:S(2)}, u32[]{:S(2)}) collective-permute-start(f32[112,128]{1,0:T(8,128)S(1)} %add_add_fusion.1), channel_id=1, source_target_pairs={{0,224},{4,228},{8,232},{12,236},{16,240},{20,244},{24,248},{28,25... | collective-permute-start | bytes 172040 | tf_op jit(solution)/shard_map/ppermute | solution.py:77
  95.8 2.6 %collective-permute-done.12 = f32[112,128]{1,0:T(8,128)S(1)} collective-permute-done((f32[112,128]{1,0:T(8,128)S(1)}, f32[112,128]{1,0:T(8,128)S(1)}, u32[]{:S(2)}, u32[]{:S(2)}) %collective-permute-start.12) | collective-permute-done | bytes 57376 | tf_op jit(solution)/shard_map/ppermute | solution.py:77
  99.4 1.8 %collective-permute-start.14 = (f32[112,128]{1,0:T(8,128)S(1)}, f32[112,128]{1,0:T(8,128)S(1)}, u32[]{:S(2)}, u32[]{:S(2)}) collective-permute-start(f32[112,128]{1,0:T(8,128)S(1)} %get-tuple-element.15), channel_id=1, source_target_pairs={{0,8},{4,12},{8,16},{12,20},{16,24},{20,28},{24,0},{28,4},{32,40},... | collective-permute-start | bytes 172040 | tf_op jit(solution)/shard_map/ppermute | solution.py:59
  105.2 2.4 %collective-permute-start.18 = (f32[448,128]{1,0:T(8,128)S(1)}, f32[448,128]{1,0:T(8,128)S(1)}, u32[]{:S(2)}, u32[]{:S(2)}) collective-permute-start(f32[448,128]{1,0:T(8,128)S(1)} %constant_dynamic-update-slice_fusion.4), channel_id=1, source_target_pairs={{0,3},{1,0},{2,1},{3,2},{4,7},{5,4},{6,5},{7,6},{8,11},{9,8},{10,9... | collective-permute-start | bytes 688136 | tf_op jit(solution)/shard_map/ppermute | solution.py:59
  107.7 3.1 %collective-permute-done.16 = f32[448,128]{1,0:T(8,128)S(1)} collective-permute-done((f32[448,128]{1,0:T(8,128)S(1)}, f32[448,128]{1,0:T(8,128)S(1)}, u32[]{:S(2)}, u32[]{:S(2)}) %collective-permute-start.16) | collective-permute-done | bytes 229408 | tf_op jit(solution)/shard_map/ppermute | solution.py:59
  110.9 2.3 %collective-permute-done.17 = f32[448,128]{1,0:T(8,128)S(1)} collective-permute-done((f32[448,128]{1,0:T(8,128)S(1)}, f32[448,128]{1,0:T(8,128)S(1)}, u32[]{:S(2)}, u32[]{:S(2)}) %collective-permute-start.17) | collective-permute-done | bytes 229408 | tf_op jit(solution)/shard_map/ppermute | solution.py:59
  113.3 8.9 %collective-permute-start.19 = (f32[1792,128]{1,0:T(8,128)S(1)}, f32[1792,128]{1,0:T(8,128)S(1)}, u32[]{:S(2)}, u32[]{:S(2)}) collective-permute-start(f32[1792,128]{1,0:T(8,128)S(1)} %constant_dynamic-update-slice_fusion), channel_id=1, source_target_pairs={{0,4},{4,0},{8,12},{12,8},{16,20},{20,16},{24,28},{28,24},{32,36},... | collective-permute-start | bytes 2752520 | tf_op jit(solution)/shard_map/ppermute | solution.py:80
  122.1 2.1 %collective-permute-done.19 = f32[1792,128]{1,0:T(8,128)S(1)} collective-permute-done((f32[1792,128]{1,0:T(8,128)S(1)}, f32[1792,128]{1,0:T(8,128)S(1)}, u32[]{:S(2)}, u32[]{:S(2)}) %collective-permute-start.19) | collective-permute-done | bytes 917536 | tf_op jit(solution)/shard_map/ppermute | solution.py:80
  124.4 39.2 %ridge_solve.1 = f32[768,112]{1,0:T(8,128)S(1)} custom-call(f32[3584,128]{1,0:T(8,128)S(1)} %maximum_select_fusion.g_ref), custom_call_target="tpu_custom_call" | custom-call | tf_op jit(solution)/shard_map/ridge_solve/pallas_call | solution.py:195
  (87 shorter events, 15.0 us)
Async XLA Ops:
  0.6 11.1 %copy-start = (bf16[1,4,240,768]{3,2,1,0:T(8,128)(2,1)S(1)}, bf16[1,4,240,768]{3,2,1,0:T(8,128)(2,1)}, u32[]{:S(2)}) copy-start(bf16[1,4,240,768]{3,2,1,0:T(8,128)(2,1)} %param.12) | copy-start | bytes 4423684
  0.7 9.9 %copy-start.3 = (f32[3072]{0:T(1024)S(1)}, f32[3072]{0:T(1024)}, u32[]{:S(2)}) copy-start(f32[3072]{0:T(1024)} %param.18) | copy-start | bytes 36868
  0.7 9.9 %copy-start.4 = (s32[1,4,240]{2,1,0:T(4,128)S(1)}, s32[1,4,240]{2,1,0:T(4,128)}, u32[]{:S(2)}) copy-start(s32[1,4,240]{2,1,0:T(4,128)} %param.22) | copy-start | bytes 11524
  0.7 10.2 %copy-start.5 = (s32[1,4,240]{2,1,0:T(4,128)S(1)}, s32[1,4,240]{2,1,0:T(4,128)}, u32[]{:S(2)}) copy-start(s32[1,4,240]{2,1,0:T(4,128)} %param.23) | copy-start | bytes 11524
  3.9 17.3 %collective-permute-start = (bf16[3,240,768]{2,1,0:T(8,128)(2,1)}, bf16[3,240,768]{2,1,0:T(8,128)(2,1)S(1)}, u32[]{:S(2)}, u32[]{:S(2)}) collective-permute-start(bf16[3,240,768]{2,1,0:T(8,128)(2,1)} %get-tuple-element.17), channel_id=1, source_target_pairs={{0,4},{4,8},{8,12},{12,16},{16,20},{20,24},{24,28},{28,32},{32,36}... | collective-permute-start | bytes 3317768 | tf_op jit(solution)/shard_map/ppermute | solution.py:449
  8.4 17.0 %collective-permute-start.1 = (bf16[3,240,768]{2,1,0:T(8,128)(2,1)}, bf16[3,240,768]{2,1,0:T(8,128)(2,1)}, u32[]{:S(2)}, u32[]{:S(2)}) collective-permute-start(bf16[3,240,768]{2,1,0:T(8,128)(2,1)} %get-tuple-element.16), channel_id=1, source_target_pairs={{4,0},{8,4},{12,8},{16,12},{20,16},{24,20},{28,24},{32,28},{36,32}... | collective-permute-start | bytes 3317768 | tf_op jit(solution)/shard_map/ppermute | solution.py:448
  54.0 2.7 %collective-permute-start.2 = (f32[1792,128]{1,0:T(8,128)S(1)}, f32[1792,128]{1,0:T(8,128)}, u32[]{:S(2)}, u32[]{:S(2)}) collective-permute-start(f32[1792,128]{1,0:T(8,128)S(1)} %constant_dynamic-slice_fusion.6), channel_id=1, source_target_pairs={{0,4},{4,0},{8,12},{12,8},{16,20},{20,16},{24,28},{28,24},{32,36},... | collective-permute-start | bytes 2752520 | tf_op jit(solution)/shard_map/ppermute | solution.py:72
  58.0 12.4 %collective-permute-start.5 = (f32[448,128]{1,0:T(8,128)S(1)}, f32[448,128]{1,0:T(8,128)S(1)}, u32[]{:S(2)}, u32[]{:S(2)}) collective-permute-start(f32[448,128]{1,0:T(8,128)S(1)} %get-tuple-element.19), channel_id=1, source_target_pairs={{0,3},{1,0},{2,1},{3,2},{4,7},{5,4},{6,5},{7,6},{8,11},{9,8},{10,9... | collective-permute-start | bytes 688136 | tf_op jit(solution)/shard_map/ppermute | solution.py:52
  60.9 12.9 %collective-permute-start.4 = (f32[448,128]{1,0:T(8,128)S(1)}, f32[448,128]{1,0:T(8,128)S(1)}, u32[]{:S(2)}, u32[]{:S(2)}) collective-permute-start(f32[448,128]{1,0:T(8,128)S(1)} %get-tuple-element.20), channel_id=1, source_target_pairs={{0,1},{1,2},{2,3},{3,0},{4,5},{5,6},{6,7},{7,4},{8,9},{9,10},{10,1... | collective-permute-start | bytes 688136 | tf_op jit(solution)/shard_map/ppermute | solution.py:52
  60.9 12.9 %collective-permute-start.3 = (f32[448,128]{1,0:T(8,128)S(1)}, f32[448,128]{1,0:T(8,128)S(1)}, u32[]{:S(2)}, u32[]{:S(2)}) collective-permute-start(f32[448,128]{1,0:T(8,128)S(1)} %get-tuple-element.18), channel_id=1, source_target_pairs={{0,2},{1,3},{2,0},{3,1},{4,6},{5,7},{6,4},{7,5},{8,10},{9,11},{10,... | collective-permute-start | bytes 688136 | tf_op jit(solution)/shard_map/ppermute | solution.py:52
  73.8 6.3 %collective-permute-start.8 = (f32[112,128]{1,0:T(8,128)S(1)}, f32[112,128]{1,0:T(8,128)S(1)}, u32[]{:S(2)}, u32[]{:S(2)}) collective-permute-start(f32[112,128]{1,0:T(8,128)S(1)} %get-tuple-element.22), channel_id=1, source_target_pairs={{0,24},{4,28},{8,0},{12,4},{16,8},{20,12},{24,16},{28,20},{32,56},... | collective-permute-start | bytes 172040 | tf_op jit(solution)/shard_map/ppermute | solution.py:52
  78.8 4.6 %collective-permute-start.7 = (f32[112,128]{1,0:T(8,128)S(1)}, f32[112,128]{1,0:T(8,128)S(1)}, u32[]{:S(2)}, u32[]{:S(2)}) collective-permute-start(f32[112,128]{1,0:T(8,128)S(1)} %get-tuple-element.23), channel_id=1, source_target_pairs={{0,8},{4,12},{8,16},{12,20},{16,24},{20,28},{24,0},{28,4},{32,40},... | collective-permute-start | bytes 172040 | tf_op jit(solution)/shard_map/ppermute | solution.py:52
  78.8 5.1 %collective-permute-start.6 = (f32[112,128]{1,0:T(8,128)S(1)}, f32[112,128]{1,0:T(8,128)S(1)}, u32[]{:S(2)}, u32[]{:S(2)}) collective-permute-start(f32[112,128]{1,0:T(8,128)S(1)} %get-tuple-element.21), channel_id=1, source_target_pairs={{0,16},{4,20},{8,24},{12,28},{16,0},{20,4},{24,8},{28,12},{32,48},... | collective-permute-start | bytes 172040 | tf_op jit(solution)/shard_map/ppermute | solution.py:52
  84.0 7.3 %collective-permute-start.10 = (f32[112,128]{1,0:T(8,128)S(1)}, f32[112,128]{1,0:T(8,128)S(1)}, u32[]{:S(2)}, u32[]{:S(2)}) collective-permute-start(f32[112,128]{1,0:T(8,128)S(1)} %add_add_fusion.2), channel_id=1, source_target_pairs={{0,64},{4,68},{8,72},{12,76},{16,80},{20,84},{24,88},{28,92},{32,9... | collective-permute-start | bytes 172040 | tf_op jit(solution)/shard_map/ppermute | solution.py:75
  87.2 6.0 %collective-permute-start.11 = (f32[112,128]{1,0:T(8,128)S(1)}, f32[112,128]{1,0:T(8,128)S(1)}, u32[]{:S(2)}, u32[]{:S(2)}) collective-permute-start(f32[112,128]{1,0:T(8,128)S(1)} %add_add_fusion.2), channel_id=1, source_target_pairs={{0,96},{4,100},{8,104},{12,108},{16,112},{20,116},{24,120},{28,124... | collective-permute-start | bytes 172040 | tf_op jit(solution)/shard_map/ppermute | solution.py:75
  91.1 3.0 %collective-permute-start.9 = (f32[112,128]{1,0:T(8,128)S(1)}, f32[112,128]{1,0:T(8,128)S(1)}, u32[]{:S(2)}, u32[]{:S(2)}) collective-permute-start(f32[112,128]{1,0:T(8,128)S(1)} %add_add_fusion.2), channel_id=1, source_target_pairs={{0,32},{4,36},{8,40},{12,44},{16,48},{20,52},{24,56},{28,60},{32,0... | collective-permute-start | bytes 172040 | tf_op jit(solution)/shard_map/ppermute | solution.py:75
  94.1 4.3 %collective-permute-start.12 = (f32[112,128]{1,0:T(8,128)S(1)}, f32[112,128]{1,0:T(8,128)S(1)}, u32[]{:S(2)}, u32[]{:S(2)}) collective-permute-start(f32[112,128]{1,0:T(8,128)S(1)} %add_add_fusion.1), channel_id=1, source_target_pairs={{0,224},{4,228},{8,232},{12,236},{16,240},{20,244},{24,248},{28,25... | collective-permute-start | bytes 172040 | tf_op jit(solution)/shard_map/ppermute | solution.py:77
  98.5 4.6 %collective-permute-start.13 = (f32[112,128]{1,0:T(8,128)S(1)}, f32[112,128]{1,0:T(8,128)S(1)}, u32[]{:S(2)}, u32[]{:S(2)}) collective-permute-start(f32[112,128]{1,0:T(8,128)S(1)} %get-tuple-element.15), channel_id=1, source_target_pairs={{0,16},{4,20},{8,24},{12,28},{16,0},{20,4},{24,8},{28,12},{32,48},... | collective-permute-start | bytes 172040 | tf_op jit(solution)/shard_map/ppermute | solution.py:59
  99.4 4.3 %collective-permute-start.14 = (f32[112,128]{1,0:T(8,128)S(1)}, f32[112,128]{1,0:T(8,128)S(1)}, u32[]{:S(2)}, u32[]{:S(2)}) collective-permute-start(f32[112,128]{1,0:T(8,128)S(1)} %get-tuple-element.15), channel_id=1, source_target_pairs={{0,8},{4,12},{8,16},{12,20},{16,24},{20,28},{24,0},{28,4},{32,40},... | collective-permute-start | bytes 172040 | tf_op jit(solution)/shard_map/ppermute | solution.py:59
  101.3 3.0 %collective-permute-start.15 = (f32[112,128]{1,0:T(8,128)S(1)}, f32[112,128]{1,0:T(8,128)S(1)}, u32[]{:S(2)}, u32[]{:S(2)}) collective-permute-start(f32[112,128]{1,0:T(8,128)S(1)} %get-tuple-element.15), channel_id=1, source_target_pairs={{0,24},{4,28},{8,0},{12,4},{16,8},{20,12},{24,16},{28,20},{32,56},... | collective-permute-start | bytes 172040 | tf_op jit(solution)/shard_map/ppermute | solution.py:59
  104.3 6.6 %collective-permute-start.16 = (f32[448,128]{1,0:T(8,128)S(1)}, f32[448,128]{1,0:T(8,128)S(1)}, u32[]{:S(2)}, u32[]{:S(2)}) collective-permute-start(f32[448,128]{1,0:T(8,128)S(1)} %constant_dynamic-update-slice_fusion.4), channel_id=1, source_target_pairs={{0,2},{1,3},{2,0},{3,1},{4,6},{5,7},{6,4},{7,5},{8,10},{9,11},{10,... | collective-permute-start | bytes 688136 | tf_op jit(solution)/shard_map/ppermute | solution.py:59
  105.0 8.3 %collective-permute-start.17 = (f32[448,128]{1,0:T(8,128)S(1)}, f32[448,128]{1,0:T(8,128)S(1)}, u32[]{:S(2)}, u32[]{:S(2)}) collective-permute-start(f32[448,128]{1,0:T(8,128)S(1)} %constant_dynamic-update-slice_fusion.4), channel_id=1, source_target_pairs={{0,1},{1,2},{2,3},{3,0},{4,5},{5,6},{6,7},{7,4},{8,9},{9,10},{10,1... | collective-permute-start | bytes 688136 | tf_op jit(solution)/shard_map/ppermute | solution.py:59
  105.2 8.0 %collective-permute-start.18 = (f32[448,128]{1,0:T(8,128)S(1)}, f32[448,128]{1,0:T(8,128)S(1)}, u32[]{:S(2)}, u32[]{:S(2)}) collective-permute-start(f32[448,128]{1,0:T(8,128)S(1)} %constant_dynamic-update-slice_fusion.4), channel_id=1, source_target_pairs={{0,3},{1,0},{2,1},{3,2},{4,7},{5,4},{6,5},{7,6},{8,11},{9,8},{10,9... | collective-permute-start | bytes 688136 | tf_op jit(solution)/shard_map/ppermute | solution.py:59
  113.3 11.0 %collective-permute-start.19 = (f32[1792,128]{1,0:T(8,128)S(1)}, f32[1792,128]{1,0:T(8,128)S(1)}, u32[]{:S(2)}, u32[]{:S(2)}) collective-permute-start(f32[1792,128]{1,0:T(8,128)S(1)} %constant_dynamic-update-slice_fusion), channel_id=1, source_target_pairs={{0,4},{4,0},{8,12},{12,8},{16,20},{20,16},{24,28},{28,24},{32,36},... | collective-permute-start | bytes 2752520 | tf_op jit(solution)/shard_map/ppermute | solution.py:80
  (7 other events, 60.7 us)
where the time goes:
time: 167 us; the launch traced here: 165 us
  Pallas kernels  75.6 us (45%)
  starting transfers between devices  42.1 us (25%)
  waiting for transfers between devices  37.1 us (22%)
  local copies, waits for them, and re-layouts  6.69 us (4%)
  other arithmetic  1.93 us (1%)
    pallas_call x1, Pallas kernels, solve(): pl.pallas_call(solve_kernel, out_shape=jax.ShapeDtypeStruct((C, BINS), F3...  39.2 us
    pallas_call x1, Pallas kernels, run_block(): pl.pallas_call(block_kernel, out_shape=(jax.ShapeDtypeStruct(own.shape, B...  28.5 us
    ppermute x6, waiting for transfers between devices, scatter4(): out = out + lax.ppermute(chunk(arr, (me + k) % 4, size), axis, pairs(k))  15.1 us
    ppermute x6, starting transfers between devices, scatter4(): out = out + lax.ppermute(chunk(arr, (me + k) % 4, size), axis, pairs(k))  10.7 us
    ppermute x1, starting transfers between devices, sum_devices(): other = lax.ppermute(arr, 'strip', CORE)  8.87 us
    pallas_call x1, Pallas kernels, run_own(): pl.pallas_call(own_kernel, out_shape=(part, was), in_specs=[pl.BlockSpec(...  7.87 us
    ppermute x6, waiting for transfers between devices, gather4(): got = [(k, lax.ppermute(arr, axis, pairs(k))) for k in (2, 1, 3)]  7.64 us
    ppermute x3, starting transfers between devices, sum_devices(): near = {m: lax.ppermute(arr, 'strip', z_flip(m)) for m in (3, 2, 1)}  7.31 us
  transfers between devices with their start and end apart: 20, of which 15 were waited for; matrix products, arithmetic and copies ran while one was open for 1% of the time, Pallas kernels for 5%

commit v1 on v0

--- a/solution.py
+++ b/solution.py
@@ -289,7 +289,7 @@
 def block_kernel(
     part, was_in, top, bot, dw, vec, b_in, spread, back, bins, counts, w_in, w_out,
     feat, packed,
-    xin, xs, dwb, acc, was, normed, hid, f_ref, odd, even, win, wout, sems,
+    xin, xs, dwb, acc, was, normed, hid, f_ref, odd, even, win, wout, fout, sems,
 ):
     copies = [
         pltpu.make_async_copy(top, xin.at[pl.ds(0, 3)], sems.at[0]),
@@ -356,10 +356,12 @@
 
     def order(m, _):
         rows = pl.ds(pl.multiple_of(m * W, W), W)
-        feat[m] = jnp.dot(back[...], f_ref[rows, :], preferred_element_type=F32).astype(BF)
+        fout[m] = jnp.dot(back[...], f_ref[rows, :], preferred_element_type=F32).astype(BF)
         return 0
 
     lax.fori_loop(0, 4, order, 0)
+    leave = pltpu.make_async_copy(fout, feat, sems.at[6])
+    leave.start()
 
     weight = jnp.where(bins[...] >= 0, counts[...], 0)
     odd_w = weight % 2
@@ -384,6 +386,7 @@
     for i in range(NB):
         packed[XY0 + i * 128 : XY0 + (i + 1) * 128, :] = xy[:, i * 128 : (i + 1) * 128]
     packed[ROWS:, :] = jnp.zeros((PACK - ROWS, 128), F32)
+    leave.wait()
 
 
 def run_own(own, dw, vec, spread):
@@ -414,7 +417,7 @@
         block_kernel,
         out_shape=(jax.ShapeDtypeStruct(own.shape, BF), jax.ShapeDtypeStruct((PACK, 128), F32)),
         in_specs=[anyspec] * 4 + [VMEM] * 7 + [anyspec] * 2,
-        out_specs=(VMEM, VMEM),
+        out_specs=(anyspec, VMEM),
         scratch_shapes=[
             pltpu.VMEM((6, W, C), BF),
             pltpu.VMEM((6, PJ, 8, C), F32),
@@ -428,7 +431,8 @@
             pltpu.VMEM((128, PIX), BF),
             pltpu.VMEM((C, HID), BF),
             pltpu.VMEM((HID, C), BF),
-            pltpu.SemaphoreType.DMA((6,)),
+            pltpu.VMEM((4, W, C), BF),
+            pltpu.SemaphoreType.DMA((7,)),
         ],
         compiler_params=pltpu.CompilerParams(vmem_limit_bytes=48 * 1024 * 1024),
         name="block",
@@ -446,7 +450,7 @@
     own = frames_in[0]
     ends = lax.axis_size("strip") - 1
     bot = lax.ppermute(own[:3], "strip", [(i + 1, i) for i in range(ends)])
-    top = lax.ppermute(own[1:], "strip", [(i, i + 1) for i in range(ends)])
+    top = lax.ppermute(lax.optimization_barrier(own)[1:], "strip", [(i, i + 1) for i in range(ends)])
     vec = jnp.stack([dw_bias, 0.5 * ln_gain, 0.5 * ln_bias, b_out, layer_scale, b_out, b_out, b_out])
     features, packed = run_block(
         own, top, bot, dw_weight.reshape(49, C), vec, 0.5 * b_in.reshape(1, HID),

time: 167 us -> 165 us (0.988); the launches traced: 165 us -> 165 us
    slice x0 -> x1, local copies, waits for them, and re-layouts: none -> 2.43 us  [per_device(): lax.optimization_barrier(own)[1:]]
    slice x1, local copies, waits for them, and re-layouts: 3.17 us -> 1.06 us  [per_device(): bot = lax.ppermute(own[:3], 'strip', [(i + 1, i) for i in range(ends)])]
where the time goes in v1:
time: 165 us
  Pallas kernels  75.6 us (46%)
  starting transfers between devices  42.2 us (26%)
  waiting for transfers between devices  37.1 us (22%)
  local copies, waits for them, and re-layouts  7.01 us (4%)
  other arithmetic  1.93 us (1%)
    pallas_call x1, Pallas kernels, solve(): pl.pallas_call(solve_kernel, out_shape=jax.ShapeDtypeStruct((C, BINS), F3...  39.2 us
    pallas_call x1, Pallas kernels, run_block(): pl.pallas_call(block_kernel, out_shape=(jax.ShapeDtypeStruct(own.shape, B...  28.5 us
    ppermute x6, waiting for transfers between devices, scatter4(): out = out + lax.ppermute(chunk(arr, (me + k) % 4, size), axis, pairs(k))  15.1 us
    ppermute x6, starting transfers between devices, scatter4(): out = out + lax.ppermute(chunk(arr, (me + k) % 4, size), axis, pairs(k))  10.7 us
    ppermute x1, starting transfers between devices, sum_devices(): other = lax.ppermute(arr, 'strip', CORE)  8.87 us
    pallas_call x1, Pallas kernels, run_own(): pl.pallas_call(own_kernel, out_shape=(part, was), in_specs=[pl.BlockSpec(...  7.87 us
    ppermute x6, waiting for transfers between devices, gather4(): got = [(k, lax.ppermute(arr, axis, pairs(k))) for k in (2, 1, 3)]  7.64 us
    ppermute x3, starting transfers between devices, sum_devices(): near = {m: lax.ppermute(arr, 'strip', z_flip(m)) for m in (3, 2, 1)}  7.31 us
  transfers between devices with their start and end apart: 20, of which 15 were waited for; matrix products, arithmetic and copies ran while one was open for 1% of the time, Pallas kernels for 5%

profile of v1, /device:TPU:1, one launch (start us, length us, event | category | flops | bytes accessed | tf_op | source)
XLA Modules:
  0.0 165.0 jit_solution(1393753640490653636)
XLA Ops:
  0.6 2.4 %slice.12 = bf16[3,240,768]{2,1,0:T(8,128)(2,1)} slice(bf16[4,240,768]{2,1,0:T(8,128)(2,1)} %bitcast.7), slice={[1:4], [0:240], [0:768]} | slice | bytes 2211840 | tf_op jit(solution)/shard_map/slice | solution.py:453
  3.1 4.6 %collective-permute-start = (bf16[3,240,768]{2,1,0:T(8,128)(2,1)}, bf16[3,240,768]{2,1,0:T(8,128)(2,1)S(1)}, u32[]{:S(2)}, u32[]{:S(2)}) collective-permute-start(bf16[3,240,768]{2,1,0:T(8,128)(2,1)} %slice.12), channel_id=1, source_target_pairs={{0,4},{4,8},{8,12},{12,16},{16,20},{20,24},{24,28},{28,32},{32,36}... | collective-permute-start | bytes 3317768 | tf_op jit(solution)/shard_map/ppermute | solution.py:453
  8.8 2.0 %collective-permute-start.1 = (bf16[3,240,768]{2,1,0:T(8,128)(2,1)}, bf16[3,240,768]{2,1,0:T(8,128)(2,1)}, u32[]{:S(2)}, u32[]{:S(2)}) collective-permute-start(bf16[3,240,768]{2,1,0:T(8,128)(2,1)} %slice_bitcast_fusion), channel_id=1, source_target_pairs={{4,0},{8,4},{12,8},{16,12},{20,16},{24,20},{28,24},{32,28},{36,32}... | collective-permute-start | bytes 3317768 | tf_op jit(solution)/shard_map/ppermute | solution.py:452
  12.1 7.9 %own_rows.1 = (f32[4,30,8,768]{3,2,1,0:T(8,128)S(1)}, bf16[960,768]{1,0:T(8,128)(2,1)S(1)}) custom-call(bf16[4,240,768]{2,1,0:T(8,128)(2,1)S(1)} %bitcast.8, f32[49,768]{1,0:T(8,128)S(1)} %reshape.16.dw, f32[8,768]{1,0:T(8,128)S(1)} %stack.26.vec, bf16[288,240]{1,0:T(8,128)(2,1)S(1)} %fusion.spread), custom_call_target="tpu_custom_call" | custom-call | flops 6000000000 | bytes 12000000 | tf_op jit(solution)/shard_map/own_rows/pallas_call | solution.py:395
  21.6 4.3 %collective-permute-done.1.bot = bf16[3,240,768]{2,1,0:T(8,128)(2,1)} collective-permute-done((bf16[3,240,768]{2,1,0:T(8,128)(2,1)}, bf16[3,240,768]{2,1,0:T(8,128)(2,1)}, u32[]{:S(2)}, u32[]{:S(2)}) %collective-permute-start.1) | collective-permute-done | bytes 1105952 | tf_op jit(solution)/shard_map/ppermute | solution.py:452
  25.9 28.5 %block.1 = (bf16[4,240,768]{2,1,0:T(8,128)(2,1)}, f32[3584,128]{1,0:T(8,128)S(1)}) custom-call(f32[4,30,8,768]{3,2,1,0:T(8,128)} %copy-done.1, bf16[960,768]{1,0:T(8,128)(2,1)S(1)} %get-tuple-element.7.was_in, bf16[3,240,768]{2,1,0:T(8,128)(2,1)S(1)} %collective-permute-done.top, bf16[3,240,768]{2,1,0:T(8,128)(2,1)} %collective-permute-done.1.bot, ...), custom_call_target="tpu_custom_call" | custom-call | tf_op jit(solution)/shard_map/block/pallas_call | solution.py:416
  54.6 2.5 %collective-permute-done.2 = f32[1792,128]{1,0:T(8,128)} collective-permute-done((f32[1792,128]{1,0:T(8,128)S(1)}, f32[1792,128]{1,0:T(8,128)}, u32[]{:S(2)}, u32[]{:S(2)}) %collective-permute-start.2) | collective-permute-done | bytes 917536 | tf_op jit(solution)/shard_map/ppermute | solution.py:72
  58.5 2.8 %collective-permute-start.5 = (f32[448,128]{1,0:T(8,128)S(1)}, f32[448,128]{1,0:T(8,128)S(1)}, u32[]{:S(2)}, u32[]{:S(2)}) collective-permute-start(f32[448,128]{1,0:T(8,128)S(1)} %get-tuple-element.17), channel_id=1, source_target_pairs={{0,3},{1,0},{2,1},{3,2},{4,7},{5,4},{6,5},{7,6},{8,11},{9,8},{10,9... | collective-permute-start | bytes 688136 | tf_op jit(solution)/shard_map/ppermute | solution.py:52
  62.9 8.0 %collective-permute-done.5 = f32[448,128]{1,0:T(8,128)S(1)} collective-permute-done((f32[448,128]{1,0:T(8,128)S(1)}, f32[448,128]{1,0:T(8,128)S(1)}, u32[]{:S(2)}, u32[]{:S(2)}) %collective-permute-start.5) | collective-permute-done | bytes 229408 | tf_op jit(solution)/shard_map/ppermute | solution.py:52
  70.9 3.3 %collective-permute-done.4 = f32[448,128]{1,0:T(8,128)S(1)} collective-permute-done((f32[448,128]{1,0:T(8,128)S(1)}, f32[448,128]{1,0:T(8,128)S(1)}, u32[]{:S(2)}, u32[]{:S(2)}) %collective-permute-start.4) | collective-permute-done | bytes 229408 | tf_op jit(solution)/shard_map/ppermute | solution.py:52
  74.3 5.0 %collective-permute-start.8 = (f32[112,128]{1,0:T(8,128)S(1)}, f32[112,128]{1,0:T(8,128)S(1)}, u32[]{:S(2)}, u32[]{:S(2)}) collective-permute-start(f32[112,128]{1,0:T(8,128)S(1)} %get-tuple-element.20), channel_id=1, source_target_pairs={{0,24},{4,28},{8,0},{12,4},{16,8},{20,12},{24,16},{28,20},{32,56},... | collective-permute-start | bytes 172040 | tf_op jit(solution)/shard_map/ppermute | solution.py:52
  80.5 3.3 %collective-permute-done.7 = f32[112,128]{1,0:T(8,128)S(1)} collective-permute-done((f32[112,128]{1,0:T(8,128)S(1)}, f32[112,128]{1,0:T(8,128)S(1)}, u32[]{:S(2)}, u32[]{:S(2)}) %collective-permute-start.7) | collective-permute-done | bytes 57376 | tf_op jit(solution)/shard_map/ppermute | solution.py:52
  84.4 3.3 %collective-permute-start.10 = (f32[112,128]{1,0:T(8,128)S(1)}, f32[112,128]{1,0:T(8,128)S(1)}, u32[]{:S(2)}, u32[]{:S(2)}) collective-permute-start(f32[112,128]{1,0:T(8,128)S(1)} %add_add_fusion.2), channel_id=1, source_target_pairs={{0,64},{4,68},{8,72},{12,76},{16,80},{20,84},{24,88},{28,92},{32,9... | collective-permute-start | bytes 172040 | tf_op jit(solution)/shard_map/ppermute | solution.py:75
  87.7 3.9 %collective-permute-start.11 = (f32[112,128]{1,0:T(8,128)S(1)}, f32[112,128]{1,0:T(8,128)S(1)}, u32[]{:S(2)}, u32[]{:S(2)}) collective-permute-start(f32[112,128]{1,0:T(8,128)S(1)} %add_add_fusion.2), channel_id=1, source_target_pairs={{0,96},{4,100},{8,104},{12,108},{16,112},{20,116},{24,120},{28,124... | collective-permute-start | bytes 172040 | tf_op jit(solution)/shard_map/ppermute | solution.py:75
  91.7 1.9 %collective-permute-done.11 = f32[112,128]{1,0:T(8,128)S(1)} collective-permute-done((f32[112,128]{1,0:T(8,128)S(1)}, f32[112,128]{1,0:T(8,128)S(1)}, u32[]{:S(2)}, u32[]{:S(2)}) %collective-permute-start.11) | collective-permute-done | bytes 57376 | tf_op jit(solution)/shard_map/ppermute | solution.py:75
  94.6 1.7 %collective-permute-start.12 = (f32[112,128]{1,0:T(8,128)S(1)}, f32[112,128]{1,0:T(8,128)S(1)}, u32[]{:S(2)}, u32[]{:S(2)}) collective-permute-start(f32[112,128]{1,0:T(8,128)S(1)} %add_add_fusion.1), channel_id=1, source_target_pairs={{0,224},{4,228},{8,232},{12,236},{16,240},{20,244},{24,248},{28,25... | collective-permute-start | bytes 172040 | tf_op jit(solution)/shard_map/ppermute | solution.py:77
  96.3 2.6 %collective-permute-done.12 = f32[112,128]{1,0:T(8,128)S(1)} collective-permute-done((f32[112,128]{1,0:T(8,128)S(1)}, f32[112,128]{1,0:T(8,128)S(1)}, u32[]{:S(2)}, u32[]{:S(2)}) %collective-permute-start.12) | collective-permute-done | bytes 57376 | tf_op jit(solution)/shard_map/ppermute | solution.py:77
  99.9 1.8 %collective-permute-start.14 = (f32[112,128]{1,0:T(8,128)S(1)}, f32[112,128]{1,0:T(8,128)S(1)}, u32[]{:S(2)}, u32[]{:S(2)}) collective-permute-start(f32[112,128]{1,0:T(8,128)S(1)} %get-tuple-element.15), channel_id=1, source_target_pairs={{0,8},{4,12},{8,16},{12,20},{16,24},{20,28},{24,0},{28,4},{32,40},... | collective-permute-start | bytes 172040 | tf_op jit(solution)/shard_map/ppermute | solution.py:59
  105.7 2.4 %collective-permute-start.18 = (f32[448,128]{1,0:T(8,128)S(1)}, f32[448,128]{1,0:T(8,128)S(1)}, u32[]{:S(2)}, u32[]{:S(2)}) collective-permute-start(f32[448,128]{1,0:T(8,128)S(1)} %constant_dynamic-update-slice_fusion.4), channel_id=1, source_target_pairs={{0,3},{1,0},{2,1},{3,2},{4,7},{5,4},{6,5},{7,6},{8,11},{9,8},{10,9... | collective-permute-start | bytes 688136 | tf_op jit(solution)/shard_map/ppermute | solution.py:59
  108.2 3.1 %collective-permute-done.16 = f32[448,128]{1,0:T(8,128)S(1)} collective-permute-done((f32[448,128]{1,0:T(8,128)S(1)}, f32[448,128]{1,0:T(8,128)S(1)}, u32[]{:S(2)}, u32[]{:S(2)}) %collective-permute-start.16) | collective-permute-done | bytes 229408 | tf_op jit(solution)/shard_map/ppermute | solution.py:59
  111.3 2.3 %collective-permute-done.17 = f32[448,128]{1,0:T(8,128)S(1)} collective-permute-done((f32[448,128]{1,0:T(8,128)S(1)}, f32[448,128]{1,0:T(8,128)S(1)}, u32[]{:S(2)}, u32[]{:S(2)}) %collective-permute-start.17) | collective-permute-done | bytes 229408 | tf_op jit(solution)/shard_map/ppermute | solution.py:59
  113.7 8.9 %collective-permute-start.19 = (f32[1792,128]{1,0:T(8,128)S(1)}, f32[1792,128]{1,0:T(8,128)S(1)}, u32[]{:S(2)}, u32[]{:S(2)}) collective-permute-start(f32[1792,128]{1,0:T(8,128)S(1)} %constant_dynamic-update-slice_fusion), channel_id=1, source_target_pairs={{0,4},{4,0},{8,12},{12,8},{16,20},{20,16},{24,28},{28,24},{32,36},... | collective-permute-start | bytes 2752520 | tf_op jit(solution)/shard_map/ppermute | solution.py:80
  122.6 2.1 %collective-permute-done.19 = f32[1792,128]{1,0:T(8,128)S(1)} collective-permute-done((f32[1792,128]{1,0:T(8,128)S(1)}, f32[1792,128]{1,0:T(8,128)S(1)}, u32[]{:S(2)}, u32[]{:S(2)}) %collective-permute-start.19) | collective-permute-done | bytes 917536 | tf_op jit(solution)/shard_map/ppermute | solution.py:80
  124.9 39.2 %ridge_solve.1 = f32[768,112]{1,0:T(8,128)S(1)} custom-call(f32[3584,128]{1,0:T(8,128)S(1)} %maximum_select_fusion.g_ref), custom_call_target="tpu_custom_call" | custom-call | tf_op jit(solution)/shard_map/ridge_solve/pallas_call | solution.py:195
  (88 shorter events, 16.1 us)
Async XLA Ops:
  0.6 10.2 %copy-start.2 = (f32[7,7,768]{2,1,0:T(8,128)S(1)}, f32[7,7,768]{2,1,0:T(8,128)}, u32[]{:S(2)}) copy-start(f32[7,7,768]{2,1,0:T(8,128)} %param.13) | copy-start | bytes 451588
  3.1 8.0 %copy-start.3 = (f32[3072]{0:T(1024)S(1)}, f32[3072]{0:T(1024)}, u32[]{:S(2)}) copy-start(f32[3072]{0:T(1024)} %param.18) | copy-start | bytes 36868
  3.1 8.0 %copy-start.4 = (s32[1,4,240]{2,1,0:T(4,128)S(1)}, s32[1,4,240]{2,1,0:T(4,128)}, u32[]{:S(2)}) copy-start(s32[1,4,240]{2,1,0:T(4,128)} %param.22) | copy-start | bytes 11524
  3.1 8.3 %copy-start.5 = (s32[1,4,240]{2,1,0:T(4,128)S(1)}, s32[1,4,240]{2,1,0:T(4,128)}, u32[]{:S(2)}) copy-start(s32[1,4,240]{2,1,0:T(4,128)} %param.23) | copy-start | bytes 11524
  3.1 18.5 %collective-permute-start = (bf16[3,240,768]{2,1,0:T(8,128)(2,1)}, bf16[3,240,768]{2,1,0:T(8,128)(2,1)S(1)}, u32[]{:S(2)}, u32[]{:S(2)}) collective-permute-start(bf16[3,240,768]{2,1,0:T(8,128)(2,1)} %slice.12), channel_id=1, source_target_pairs={{0,4},{4,8},{8,12},{12,16},{16,20},{20,24},{24,28},{28,32},{32,36}... | collective-permute-start | bytes 3317768 | tf_op jit(solution)/shard_map/ppermute | solution.py:453
  8.8 17.0 %collective-permute-start.1 = (bf16[3,240,768]{2,1,0:T(8,128)(2,1)}, bf16[3,240,768]{2,1,0:T(8,128)(2,1)}, u32[]{:S(2)}, u32[]{:S(2)}) collective-permute-start(bf16[3,240,768]{2,1,0:T(8,128)(2,1)} %slice_bitcast_fusion), channel_id=1, source_target_pairs={{4,0},{8,4},{12,8},{16,12},{20,16},{24,20},{28,24},{32,28},{36,32}... | collective-permute-start | bytes 3317768 | tf_op jit(solution)/shard_map/ppermute | solution.py:452
  54.5 2.7 %collective-permute-start.2 = (f32[1792,128]{1,0:T(8,128)S(1)}, f32[1792,128]{1,0:T(8,128)}, u32[]{:S(2)}, u32[]{:S(2)}) collective-permute-start(f32[1792,128]{1,0:T(8,128)S(1)} %constant_dynamic-slice_fusion.6), channel_id=1, source_target_pairs={{0,4},{4,0},{8,12},{12,8},{16,20},{20,16},{24,28},{28,24},{32,36},... | collective-permute-start | bytes 2752520 | tf_op jit(solution)/shard_map/ppermute | solution.py:72
  58.5 12.4 %collective-permute-start.5 = (f32[448,128]{1,0:T(8,128)S(1)}, f32[448,128]{1,0:T(8,128)S(1)}, u32[]{:S(2)}, u32[]{:S(2)}) collective-permute-start(f32[448,128]{1,0:T(8,128)S(1)} %get-tuple-element.17), channel_id=1, source_target_pairs={{0,3},{1,0},{2,1},{3,2},{4,7},{5,4},{6,5},{7,6},{8,11},{9,8},{10,9... | collective-permute-start | bytes 688136 | tf_op jit(solution)/shard_map/ppermute | solution.py:52
  61.3 12.9 %collective-permute-start.4 = (f32[448,128]{1,0:T(8,128)S(1)}, f32[448,128]{1,0:T(8,128)S(1)}, u32[]{:S(2)}, u32[]{:S(2)}) collective-permute-start(f32[448,128]{1,0:T(8,128)S(1)} %get-tuple-element.18), channel_id=1, source_target_pairs={{0,1},{1,2},{2,3},{3,0},{4,5},{5,6},{6,7},{7,4},{8,9},{9,10},{10,1... | collective-permute-start | bytes 688136 | tf_op jit(solution)/shard_map/ppermute | solution.py:52
  61.3 12.9 %collective-permute-start.3 = (f32[448,128]{1,0:T(8,128)S(1)}, f32[448,128]{1,0:T(8,128)S(1)}, u32[]{:S(2)}, u32[]{:S(2)}) collective-permute-start(f32[448,128]{1,0:T(8,128)S(1)} %get-tuple-element.16), channel_id=1, source_target_pairs={{0,2},{1,3},{2,0},{3,1},{4,6},{5,7},{6,4},{7,5},{8,10},{9,11},{10,... | collective-permute-start | bytes 688136 | tf_op jit(solution)/shard_map/ppermute | solution.py:52
  74.3 6.3 %collective-permute-start.8 = (f32[112,128]{1,0:T(8,128)S(1)}, f32[112,128]{1,0:T(8,128)S(1)}, u32[]{:S(2)}, u32[]{:S(2)}) collective-permute-start(f32[112,128]{1,0:T(8,128)S(1)} %get-tuple-element.20), channel_id=1, source_target_pairs={{0,24},{4,28},{8,0},{12,4},{16,8},{20,12},{24,16},{28,20},{32,56},... | collective-permute-start | bytes 172040 | tf_op jit(solution)/shard_map/ppermute | solution.py:52
  79.3 4.6 %collective-permute-start.7 = (f32[112,128]{1,0:T(8,128)S(1)}, f32[112,128]{1,0:T(8,128)S(1)}, u32[]{:S(2)}, u32[]{:S(2)}) collective-permute-start(f32[112,128]{1,0:T(8,128)S(1)} %get-tuple-element.21), channel_id=1, source_target_pairs={{0,8},{4,12},{8,16},{12,20},{16,24},{20,28},{24,0},{28,4},{32,40},... | collective-permute-start | bytes 172040 | tf_op jit(solution)/shard_map/ppermute | solution.py:52
  79.3 5.1 %collective-permute-start.6 = (f32[112,128]{1,0:T(8,128)S(1)}, f32[112,128]{1,0:T(8,128)S(1)}, u32[]{:S(2)}, u32[]{:S(2)}) collective-permute-start(f32[112,128]{1,0:T(8,128)S(1)} %get-tuple-element.19), channel_id=1, source_target_pairs={{0,16},{4,20},{8,24},{12,28},{16,0},{20,4},{24,8},{28,12},{32,48},... | collective-permute-start | bytes 172040 | tf_op jit(solution)/shard_map/ppermute | solution.py:52
  84.4 7.3 %collective-permute-start.10 = (f32[112,128]{1,0:T(8,128)S(1)}, f32[112,128]{1,0:T(8,128)S(1)}, u32[]{:S(2)}, u32[]{:S(2)}) collective-permute-start(f32[112,128]{1,0:T(8,128)S(1)} %add_add_fusion.2), channel_id=1, source_target_pairs={{0,64},{4,68},{8,72},{12,76},{16,80},{20,84},{24,88},{28,92},{32,9... | collective-permute-start | bytes 172040 | tf_op jit(solution)/shard_map/ppermute | solution.py:75
  87.7 6.0 %collective-permute-start.11 = (f32[112,128]{1,0:T(8,128)S(1)}, f32[112,128]{1,0:T(8,128)S(1)}, u32[]{:S(2)}, u32[]{:S(2)}) collective-permute-start(f32[112,128]{1,0:T(8,128)S(1)} %add_add_fusion.2), channel_id=1, source_target_pairs={{0,96},{4,100},{8,104},{12,108},{16,112},{20,116},{24,120},{28,124... | collective-permute-start | bytes 172040 | tf_op jit(solution)/shard_map/ppermute | solution.py:75
  91.5 3.0 %collective-permute-start.9 = (f32[112,128]{1,0:T(8,128)S(1)}, f32[112,128]{1,0:T(8,128)S(1)}, u32[]{:S(2)}, u32[]{:S(2)}) collective-permute-start(f32[112,128]{1,0:T(8,128)S(1)} %add_add_fusion.2), channel_id=1, source_target_pairs={{0,32},{4,36},{8,40},{12,44},{16,48},{20,52},{24,56},{28,60},{32,0... | collective-permute-start | bytes 172040 | tf_op jit(solution)/shard_map/ppermute | solution.py:75
  94.6 4.3 %collective-permute-start.12 = (f32[112,128]{1,0:T(8,128)S(1)}, f32[112,128]{1,0:T(8,128)S(1)}, u32[]{:S(2)}, u32[]{:S(2)}) collective-permute-start(f32[112,128]{1,0:T(8,128)S(1)} %add_add_fusion.1), channel_id=1, source_target_pairs={{0,224},{4,228},{8,232},{12,236},{16,240},{20,244},{24,248},{28,25... | collective-permute-start | bytes 172040 | tf_op jit(solution)/shard_map/ppermute | solution.py:77
  98.9 4.6 %collective-permute-start.13 = (f32[112,128]{1,0:T(8,128)S(1)}, f32[112,128]{1,0:T(8,128)S(1)}, u32[]{:S(2)}, u32[]{:S(2)}) collective-permute-start(f32[112,128]{1,0:T(8,128)S(1)} %get-tuple-element.15), channel_id=1, source_target_pairs={{0,16},{4,20},{8,24},{12,28},{16,0},{20,4},{24,8},{28,12},{32,48},... | collective-permute-start | bytes 172040 | tf_op jit(solution)/shard_map/ppermute | solution.py:59
  99.9 4.3 %collective-permute-start.14 = (f32[112,128]{1,0:T(8,128)S(1)}, f32[112,128]{1,0:T(8,128)S(1)}, u32[]{:S(2)}, u32[]{:S(2)}) collective-permute-start(f32[112,128]{1,0:T(8,128)S(1)} %get-tuple-element.15), channel_id=1, source_target_pairs={{0,8},{4,12},{8,16},{12,20},{16,24},{20,28},{24,0},{28,4},{32,40},... | collective-permute-start | bytes 172040 | tf_op jit(solution)/shard_map/ppermute | solution.py:59
  101.7 3.0 %collective-permute-start.15 = (f32[112,128]{1,0:T(8,128)S(1)}, f32[112,128]{1,0:T(8,128)S(1)}, u32[]{:S(2)}, u32[]{:S(2)}) collective-permute-start(f32[112,128]{1,0:T(8,128)S(1)} %get-tuple-element.15), channel_id=1, source_target_pairs={{0,24},{4,28},{8,0},{12,4},{16,8},{20,12},{24,16},{28,20},{32,56},... | collective-permute-start | bytes 172040 | tf_op jit(solution)/shard_map/ppermute | solution.py:59
  104.7 6.6 %collective-permute-start.16 = (f32[448,128]{1,0:T(8,128)S(1)}, f32[448,128]{1,0:T(8,128)S(1)}, u32[]{:S(2)}, u32[]{:S(2)}) collective-permute-start(f32[448,128]{1,0:T(8,128)S(1)} %constant_dynamic-update-slice_fusion.4), channel_id=1, source_target_pairs={{0,2},{1,3},{2,0},{3,1},{4,6},{5,7},{6,4},{7,5},{8,10},{9,11},{10,... | collective-permute-start | bytes 688136 | tf_op jit(solution)/shard_map/ppermute | solution.py:59
  105.4 8.3 %collective-permute-start.17 = (f32[448,128]{1,0:T(8,128)S(1)}, f32[448,128]{1,0:T(8,128)S(1)}, u32[]{:S(2)}, u32[]{:S(2)}) collective-permute-start(f32[448,128]{1,0:T(8,128)S(1)} %constant_dynamic-update-slice_fusion.4), channel_id=1, source_target_pairs={{0,1},{1,2},{2,3},{3,0},{4,5},{5,6},{6,7},{7,4},{8,9},{9,10},{10,1... | collective-permute-start | bytes 688136 | tf_op jit(solution)/shard_map/ppermute | solution.py:59
  105.7 8.0 %collective-permute-start.18 = (f32[448,128]{1,0:T(8,128)S(1)}, f32[448,128]{1,0:T(8,128)S(1)}, u32[]{:S(2)}, u32[]{:S(2)}) collective-permute-start(f32[448,128]{1,0:T(8,128)S(1)} %constant_dynamic-update-slice_fusion.4), channel_id=1, source_target_pairs={{0,3},{1,0},{2,1},{3,2},{4,7},{5,4},{6,5},{7,6},{8,11},{9,8},{10,9... | collective-permute-start | bytes 688136 | tf_op jit(solution)/shard_map/ppermute | solution.py:59
  113.7 11.0 %collective-permute-start.19 = (f32[1792,128]{1,0:T(8,128)S(1)}, f32[1792,128]{1,0:T(8,128)S(1)}, u32[]{:S(2)}, u32[]{:S(2)}) collective-permute-start(f32[1792,128]{1,0:T(8,128)S(1)} %constant_dynamic-update-slice_fusion), channel_id=1, source_target_pairs={{0,4},{4,0},{8,12},{12,8},{16,20},{20,16},{24,28},{28,24},{32,36},... | collective-permute-start | bytes 2752520 | tf_op jit(solution)/shard_map/ppermute | solution.py:80
  (7 other events, 48.2 us)
